TPU v7x, 32 devices: a whole 2x2x4 slice. The times are simulated.
32 devices in a mesh: groups: 2 (over x), sub: 16 (over z, y, core).
Axes of the slice: x: 2, y: 2, z: 4, core: 2. Of those that a mesh axis runs over, the one named last changes fastest.
Arguments:
- modes_start: float32 [48, 6, 8192], P(None, None, ('groups', 'sub')), parts along dimension 2, may hold values from -6 to 6
- stiffness: float32 [24, 24, 8192], P(None, None, ('groups', 'sub')), parts along dimension 2, as said below
- mass: float32 [24, 24, 8192], P(None, None, ('groups', 'sub')), parts along dimension 2, as said below
- connect: int32 [4, 8192], P(None, ('groups', 'sub')), parts along dimension 1, may hold values from 0 to 382, as said below
Outputs:
- modes: float32 [48, 6, 8192], P(None, None, ('groups', 'sub')), parts along dimension 2
- ritz: float32 [96], P('groups'), parts along dimension 0
There are 2 independent parts, one for each index of `groups`. A program takes and returns all parts, laid end to end along the dimension named above; each array names one. Nothing has to cross between parts.
Inputs may be any that keep to these rules, and one draw needn't show every extreme that they name: `connect`: for element l of a subdomain, the four nodes are l + 64, one above it by less than 32, one below it by at most 64, and one above it by 32 or more and less than 64. `stiffness`: each block is symmetric positive definite. `mass`: each block is symmetric positive definite.
All inputs are finite; a program needn't handle non-finite values.
Results may differ from a plain program's by a relative error of at most 0.0001.
Values sent between devices are 32-bit elements; how exact they have to be, the bound alone decides.
No kernel may reach another device: no remote copies, remote signals or barrier semaphores. Data moves between devices by JAX's collectives and lax.ppermute only.
A program may use at most 64 MiB of HBM per device.

v0:
```python
import jax
import jax.numpy as jnp
from jax import lax
from jax.sharding import PartitionSpec as P

MODES = 48
HALO = 64
ITERS = 2
SMALL_STEPS = 2
highest = lax.Precision.HIGHEST


def with_halo(block, sides, width):
    for axis, dim in sides:
        count = lax.axis_size(axis)
        forward = [(i, i + 1) for i in range(count - 1)]
        backward = [(target, source) for source, target in forward]
        low = lax.ppermute(
            lax.slice_in_dim(block, block.shape[dim] - width, None, axis=dim), axis, forward
        )
        high = lax.ppermute(lax.slice_in_dim(block, 0, width, axis=dim), axis, backward)
        block = jnp.concatenate([low, block, high], axis=dim)
    return block


def shifted(value, axis, steps):
    count = lax.axis_size(axis)
    initial, last = (max(0, -steps), min(count, count - steps))
    return lax.ppermute(value, axis, [(source, source + steps) for source in range(initial, last)])


def inner(left, right):
    return jnp.einsum("acn,bcn->ab", left, right, precision=highest)


def combine(coeff, block):
    return jnp.einsum("ab,bcn->acn", coeff, block, precision=highest)


def symmetric(matrix):
    return 0.5 * (matrix + matrix.T)


def lower_solve(factor, rhs, transpose):
    return lax.linalg.triangular_solve(
        factor, rhs, left_side=True, lower=True, transpose_a=transpose
    )


def small_step(stiff_gram, mass_gram):
    scaling = 1.0 / jnp.sqrt(jnp.diagonal(mass_gram))
    outer = scaling[:, None] * scaling[None, :]
    stiff_scaled = symmetric(stiff_gram * outer)
    mass_scaled = symmetric(mass_gram * outer)
    factor = jnp.linalg.cholesky(stiff_scaled)
    coeff = jnp.eye(stiff_gram.shape[0], MODES, dtype=stiff_gram.dtype)
    for sweep in range(SMALL_STEPS):
        pushed = jnp.dot(mass_scaled, coeff, precision=highest)
        solved = lower_solve(factor, lower_solve(factor, pushed, False), True)
        normal_gram = symmetric(
            jnp.dot(solved.T, jnp.dot(mass_scaled, solved, precision=highest), precision=highest)
        )
        small_factor = jnp.linalg.cholesky(normal_gram)
        coeff = lower_solve(small_factor, solved.T, False).T
    return coeff * scaling[:, None]


def apply_pair(block, stiffness, mass, connect):
    rows = block.shape[0]
    count = block.shape[2]
    extended = with_halo(block, (("sub", 2),), HALO)
    width = count + 2 * HALO
    span = 128
    blocks = count // span
    window = span + 2 * HALO
    positions = jnp.arange(window, dtype=jnp.int32)
    stiff_blocks = stiffness.reshape(24, 24, blocks, span).transpose(2, 0, 1, 3)
    mass_blocks = mass.reshape(24, 24, blocks, span).transpose(2, 0, 1, 3)
    link_blocks = connect.reshape(4, blocks, span).transpose(1, 0, 2)

    def one_block(total, inputs):
        index, stiff_here, mass_here, link_here = inputs
        start = index * span
        local_window = lax.dynamic_slice_in_dim(extended, start, window, 2)
        selector = (link_here[:, :, None] - start == positions[None, None, :]).astype(block.dtype)
        picked = jnp.einsum("rcw,aew->rcae", local_window, selector, precision=highest).reshape(
            rows, 24, span
        )
        stiff_part = jnp.einsum("ije,rje->rie", stiff_here, picked, precision=highest)
        mass_part = jnp.einsum("ije,rje->rie", mass_here, picked, precision=highest)
        parts = jnp.stack([stiff_part, mass_part]).reshape(2, rows, 6, 4, span)
        placed = jnp.einsum("xrcae,aew->xrcw", parts, selector, precision=highest)
        old = lax.dynamic_slice_in_dim(total, start, window, 3)
        return (lax.dynamic_update_slice_in_dim(total, old + placed, start, 3), None)

    initial = jnp.zeros((2, rows, 6, width), block.dtype)
    summed, unused = lax.scan(
        one_block,
        initial,
        (jnp.arange(blocks, dtype=jnp.int32), stiff_blocks, mass_blocks, link_blocks),
    )
    from_below = shifted(summed[:, :, :, count + HALO :], "sub", 1)
    from_above = shifted(summed[:, :, :, :HALO], "sub", -1)
    inside = summed[:, :, :, HALO : count + HALO]
    inside = inside.at[:, :, :, :HALO].add(from_below)
    inside = inside.at[:, :, :, count - HALO :].add(from_above)
    return (inside[0], inside[1])


def body(modes_start, stiffness, mass, connect):
    stiff_start, mass_start = apply_pair(modes_start, stiffness, mass, connect)
    stiff_proj, mass_proj = lax.psum(
        (inner(modes_start, stiff_start), inner(modes_start, mass_start)), "sub"
    )
    factor = jnp.linalg.cholesky(symmetric(mass_proj))
    inverse = lower_solve(factor, jnp.eye(MODES, dtype=mass_proj.dtype), False)
    current = combine(inverse, modes_start)
    stiff_cur = combine(inverse, stiff_start)
    mass_cur = combine(inverse, mass_start)
    rayleigh = symmetric(
        jnp.dot(inverse, jnp.dot(stiff_proj, inverse.T, precision=highest), precision=highest)
    )
    direction = current
    stiff_dir = current
    mass_dir = current
    carried = rayleigh
    for sweep in range(ITERS):
        if sweep > 0:
            rayleigh = symmetric(lax.psum(inner(current, stiff_cur), "sub"))
        residual = stiff_cur - combine(rayleigh, mass_cur)
        stiff_res, mass_res = apply_pair(residual, stiffness, mass, connect)
        if sweep == 0:
            basis = jnp.concatenate([current, residual])
            stiff_basis = jnp.concatenate([stiff_cur, stiff_res])
            mass_basis = jnp.concatenate([mass_cur, mass_res])
        else:
            basis = jnp.concatenate([current, residual, direction])
            stiff_basis = jnp.concatenate([stiff_cur, stiff_res, stiff_dir])
            mass_basis = jnp.concatenate([mass_cur, mass_res, mass_dir])
        stiff_gram, mass_gram = lax.psum(
            (inner(basis, stiff_basis), inner(basis, mass_basis)), "sub"
        )
        coeff = small_step(stiff_gram, mass_gram)
        carried = symmetric(
            jnp.dot(coeff.T, jnp.dot(stiff_gram, coeff, precision=highest), precision=highest)
        )
        current = combine(coeff.T, basis)
        direction = combine(coeff[MODES:].T, basis[MODES:])
        if sweep + 1 < ITERS:
            stiff_cur = combine(coeff.T, stiff_basis)
            mass_cur = combine(coeff.T, mass_basis)
            stiff_dir = combine(coeff[MODES:].T, stiff_basis[MODES:])
            mass_dir = combine(coeff[MODES:].T, mass_basis[MODES:])
    return (current, jnp.diagonal(carried))


def solution(mesh):
    in_specs = (
        P(None, None, ("groups", "sub")),
        P(None, None, ("groups", "sub")),
        P(None, None, ("groups", "sub")),
        P(None, ("groups", "sub")),
    )
    out_specs = (P(None, None, ("groups", "sub")), P("groups"))
    return jax.shard_map(body, mesh=mesh, in_specs=in_specs, out_specs=out_specs, check_vma=False)
```

profile of v0, /device:TPU:0, one launch (start us, length us, event | category | flops | bytes accessed | tf_op | source)
XLA Modules:
  0.0 624.3 jit_solution(5031614352455597482)
XLA Ops:
  8.3 2.4 collective-permute-start
  12.2 3.1 copy.66
  15.2 2.2 copy.67
  19.5 33.1 %while.45 = (s32[]{:T(128)}, f32[2,48,6,384]{3,1,2,0:T(8,128)}, s32[2]{0:T(128)S(1)}, f32[48,6,384]{2,0,1:T(8,128)}, s32[2,4,128]{2,1,0:T(4,128)S(1)}, /*index=5...) while((s32[]{:T(128)}, f32[2,48,6,384]{3,1,2,0:T(8,128)}, ...), condition=%wide.region_1.2_spmd.clone, body=%wide.region_0.1_spmd.clone.sunk | while | flops 1444594176 | bytes 14656723 | solution.py:97
  20.7 1.5 fusion.318
  22.8 4.0 fusion.320
  28.2 4.0 fusion.319
  33.3 2.7 fusion.321
  37.3 1.5 fusion.318
  39.3 4.0 fusion.320
  44.8 4.0 fusion.319
  49.9 2.7 fusion.321
  53.9 5.2 collective-permute-start.2
  61.3 2.7 collective-permute-done.3
  64.1 2.3 scatter-add.21
  67.2 63.9 %all-reduce.6 = (f32[48,48]{1,0:T(8,128)S(1)}, f32[48,48]{0,1:T(8,128)S(1)}) all-reduce(f32[48,48]{1,0:T(8,128)S(1)} %convolution_bitcast_fusion.9, f32[48,48]{0,1:T(8,128)S(1)} %convolution_bitcast_fusion.8), channel_id=1, replica_groups=mesh['groups'=2,'sub'=16] {'sub'}, use_global_device_ids=true, to_apply=%region_2.3 | all-reduce | flops 4608 | bytes 36864 | tf_op jit(solution)/shard_map/psum | solution.py:112
  131.3 4.4 cholesky.251
  137.0 3.7 custom-call.37
  145.3 1.9 collective-permute-done.5
  148.5 31.3 %while.46 = (s32[]{:T(128)}, f32[2,48,6,384]{3,1,2,0:T(8,128)}, s32[2]{0:T(128)S(1)}, f32[48,6,384]{2,0,1:T(8,128)S(1)}, s32[2,4,128]{2,1,0:T(4,128)S(1)}, /*ind...) while((s32[]{:T(128)}, f32[2,48,6,384]{3,1,2,0:T(8,128)}, ...), condition=%wide.region_7.9_spmd.clone, body=%wide.region_6.8_spmd.clone.sunk | while | flops 1444594176 | bytes 18195724 | solution.py:97
  151.0 4.0 fusion.332
  156.4 4.0 fusion.331
  161.5 2.7 fusion.333
  166.6 4.0 fusion.332
  172.0 4.0 fusion.331
  177.2 2.7 fusion.333
  181.1 2.9 collective-permute-start.6
  185.6 1.5 collective-permute-start.7
  189.3 2.3 scatter-add.25
  194.2 91.6 %all-reduce.11.cloned.1.call-done = (f32[96,96]{0,1:T(8,128)}, f32[96,96]{0,1:T(8,128)}) async-done(((f32[96,96]{0,1:T(8,128)}, f32[96,96]{0,1:T(8,128)}), (f32[96,96]{0,1:T(8,128)}, f32[96,96]{0,1:T(8,128)})) %all-reduce.11.cloned.1.call-update) | async-done | bytes 73744 | tf_op jit(solution)/shard_map/psum | solution.py:140
  285.8 2.2 gather_fusion
  289.3 8.8 %cholesky.95 = f32[96,96]{1,0:T(8,128)S(1)} custom-call(f32[96,96]{1,0:T(8,128)S(1)} %broadcast_multiply_fusion.1), custom_call_target="Cholesky" | custom-call | tf_op jit(solution)/shard_map/jit(cholesky)/cholesky | solution.py:55
  299.4 7.4 %custom-call.55 = f32[1,96,96]{1,2,0:T(8,128)S(1)} custom-call(f32[1,96,96]{2,1,0:T(8,128)S(1)} %fusion.104), custom_call_target="InvertDiagBlocksLowerTriangular" | custom-call | tf_op jit(solution)/shard_map/triangular_solve/custom-call.7 | solution.py:45
  308.1 4.4 cholesky.262
  313.8 3.7 custom-call.53
  319.0 4.4 cholesky.273
  324.7 3.7 custom-call.56
  331.5 58.5 %psum.53 = f32[48,48]{1,0:T(8,128)S(1)} all-reduce(f32[48,48]{1,0:T(8,128)S(1)} %convolution_bitcast_fusion.7), channel_id=1, replica_groups=mesh['groups'=2,'sub'=16] {'sub'}, use_global_device_ids=true, to_apply=%region_12.17 | all-reduce | flops 2304 | bytes 18432 | tf_op jit(solution)/shard_map/psum | solution.py:129
  392.0 1.5 collective-permute-start.9
  397.2 33.2 %while.47 = (s32[]{:T(128)}, f32[2,48,6,384]{3,1,2,0:T(8,128)}, s32[2]{0:T(128)S(1)}, f32[48,6,384]{2,0,1:T(8,128)}, s32[2,4,128]{2,1,0:T(4,128)S(1)}, /*index=5...) while((s32[]{:T(128)}, f32[2,48,6,384]{3,1,2,0:T(8,128)}, ...), condition=%wide.region_14.19_spmd.clone, body=%wide.region_13.18_spmd.clone.sunk | while | flops 1444594176 | bytes 14656723 | solution.py:97
  398.5 1.5 fusion.342
  400.6 4.0 fusion.344
  406.0 4.0 fusion.343
  411.2 2.7 fusion.345
  415.1 1.5 fusion.342
  417.2 4.0 fusion.344
  422.7 4.0 fusion.343
  427.8 2.7 fusion.345
  431.7 2.9 collective-permute-start.10
  436.3 1.7 collective-permute-start.11
  439.9 2.3 scatter-add.29
  442.3 1.5 convolution_bitcast_fusion.3
  443.8 1.5 convolution_bitcast_fusion.4
  445.4 93.9 %all-reduce.13.cloned.1.call-done = (f32[144,144]{0,1:T(8,128)}, f32[144,144]{0,1:T(8,128)}) async-done(((f32[144,144]{0,1:T(8,128)}, f32[144,144]{0,1:T(8,128)}), (f32[144,144]{0,1:T(8,128)}, f32[144,144]{0,1:T(8,128)})) %all-reduce.13.cloned.1.call-update) | async-done | bytes 165904 | tf_op jit(solution)/shard_map/psum | solution.py:140
  539.3 3.2 gather_fusion.1
  544.4 11.7 %cholesky.155 = f32[128,128]{1,0:T(8,128)S(1)} custom-call(f32[128,128]{1,0:T(8,128)S(1)} %cholesky.304), custom_call_target="Cholesky" | custom-call | tf_op jit(solution)/shard_map/jit(cholesky)/cholesky | solution.py:55
  556.2 9.8 %custom-call.38 = f32[1,128,128]{1,2,0:T(8,128)S(1)} custom-call(f32[1,128,128]{2,1,0:T(8,128)S(1)} %get-tuple-element.375), custom_call_target="InvertDiagBlocksLowerTriangular" | custom-call | tf_op jit(solution)/shard_map/jit(cholesky)/cholesky | solution.py:55
  566.3 1.5 cholesky.175
  570.6 19.8 %custom-call.61 = f32[2,128,128]{1,2,0:T(8,128)S(1)} custom-call(f32[2,128,128]{2,1,0:T(8,128)S(1)} %pad_maximum_fusion.17), custom_call_target="InvertDiagBlocksLowerTriangular" | custom-call | tf_op jit(solution)/shard_map/triangular_solve/custom-call.10 | solution.py:45
  592.3 4.4 cholesky.284
  598.0 3.7 custom-call.59
  604.1 4.4 cholesky.295
  609.8 3.7 custom-call.62
  615.9 1.5 gather_fusion.2
  (279 shorter events, 80.6 us)
Async XLA Ops:
  7.2 278.7 %all-reduce.11.cloned.1.call-start = ((), (), s32[]{:S(2)}) async-start(), calls=%async_computation | async-start | bytes 196608 | tf_op jit(solution)/shard_map/psum | solution.py:140
  8.3 9.2 %collective-permute-start = (f32[48,6,64]{2,0,1:T(8,128)S(1)}, f32[48,6,64]{2,0,1:T(8,128)S(1)}, u32[]{:S(2)}, u32[]{:S(2)}) collective-permute-start(f32[48,6,64]{2,0,1:T(8,128)S(1)} %get-tuple-element.372), channel_id=1, source_target_pairs={{0,1},{1,2},{2,3},{3,4},{4,5},{5,6},{6,7},{7,8},{8,9},{9,10},{10,1... | collective-permute-start | bytes 221192 | tf_op jit(solution)/shard_map/ppermute | solution.py:18
  10.7 4.5 copy-start.23
  10.7 6.7 %collective-permute-start.1 = (f32[48,6,64]{2,0,1:T(8,128)S(1)}, f32[48,6,64]{2,0,1:T(8,128)S(1)}, u32[]{:S(2)}, u32[]{:S(2)}) collective-permute-start(f32[48,6,64]{2,0,1:T(8,128)S(1)} %get-tuple-element.373), channel_id=1, source_target_pairs={{1,0},{2,1},{3,2},{4,3},{5,4},{6,5},{7,6},{8,7},{9,8},{10,9},{11,1... | collective-permute-start | bytes 221192 | tf_op jit(solution)/shard_map/ppermute | solution.py:21
  15.2 2.2 copy-start.8
  17.5 2.0 copy-start.26
  32.3 1.1 copy-start
  48.8 1.1 copy-start
  52.6 6.5 %copy-start.3 = (f32[2,48,6,384]{3,1,2,0:T(8,128)S(1)}, f32[2,48,6,384]{3,1,2,0:T(8,128)}, u32[]{:S(2)}) copy-start(f32[2,48,6,384]{3,1,2,0:T(8,128)} %get-tuple-element.207) | copy-start | bytes 2654212
  53.9 6.7 %collective-permute-start.2 = (f32[2,48,6,64]{3,1,2,0:T(8,128)S(1)}, f32[2,48,6,64]{3,1,2,0:T(8,128)S(1)}, u32[]{:S(2)}, u32[]{:S(2)}) collective-permute-start(f32[2,48,6,64]{3,1,2,0:T(8,128)S(1)} %get-tuple-element.363), channel_id=1, source_target_pairs={{0,1},{1,2},{2,3},{3,4},{4,5},{5,6},{6,7},{7,8},{8,9},{9,10},{10,1... | collective-permute-start | bytes 442376 | tf_op jit(solution)/shard_map/ppermute | solution.py:29
  59.3 4.7 collective-permute-start.3
  141.3 6.2 copy-start.10
  141.7 6.8 %copy-start.12 = (f32[48,6,256]{2,0,1:T(8,128)}, f32[48,6,256]{2,0,1:T(8,128)S(1)}, u32[]{:S(2)}) copy-start(f32[48,6,256]{2,0,1:T(8,128)S(1)} %fusion.93) | copy-start | bytes 884740
  142.7 2.6 collective-permute-start.4
  144.0 3.3 collective-permute-start.5
  148.5 2.4 copy-start.6
  160.4 1.1 copy-start.1
  161.1 3.1 copy-start.7
  164.2 2.4 copy-start.6
  176.1 1.1 copy-start.1
  176.8 3.1 copy-start.7
  179.9 5.6 copy-start.4
  181.1 6.0 collective-permute-start.6
  185.6 3.5 collective-permute-start.7
  187.3 4.3 copy-start.13
  189.3 3.6 copy-start.11
  191.5 138.4 %copy-start.9 = (f32[2,48,6,256]{3,1,2,0:T(8,128)}, f32[2,48,6,256]{3,1,2,0:T(8,128)S(1)}, u32[]{:S(2)}) copy-start(f32[2,48,6,256]{3,1,2,0:T(8,128)S(1)} %scatter-add.25) | copy-start | bytes 1769476
  194.1 345.2 %all-reduce.13.cloned.1.call-start = ((), (), s32[]{:S(2)}) async-start(), calls=%async_computation.1 | async-start | bytes 589824 | tf_op jit(solution)/shard_map/psum | solution.py:140
  329.1 61.0 %copy-start.18 = (f32[48,6,256]{2,0,1:T(8,128)}, f32[48,6,256]{2,0,1:T(8,128)S(1)}, u32[]{:S(2)}) copy-start(f32[48,6,256]{2,0,1:T(8,128)S(1)} %fusion.90) | copy-start | bytes 884740
  329.5 61.0 %copy-start.16 = (f32[48,6,256]{2,0,1:T(8,128)}, f32[48,6,256]{2,0,1:T(8,128)S(1)}, u32[]{:S(2)}) copy-start(f32[48,6,256]{2,0,1:T(8,128)S(1)} %fusion.89) | copy-start | bytes 884740
  330.0 64.7 %copy-start.20 = (f32[48,6,256]{2,0,1:T(8,128)}, f32[48,6,256]{2,0,1:T(8,128)S(1)}, u32[]{:S(2)}) copy-start(f32[48,6,256]{2,0,1:T(8,128)S(1)} %fusion.88) | copy-start | bytes 884740
  390.5 4.7 copy-start.14
  390.7 4.0 collective-permute-start.8
  392.0 3.3 collective-permute-start.9
  410.1 1.1 copy-start.2
  426.7 1.1 copy-start.2
  430.5 5.6 copy-start.5
  431.7 6.3 %collective-permute-start.10 = (f32[2,48,6,64]{3,1,2,0:T(8,128)S(1)}, f32[2,48,6,64]{3,1,2,0:T(8,128)S(1)}, u32[]{:S(2)}, u32[]{:S(2)}) collective-permute-start(f32[2,48,6,64]{3,1,2,0:T(8,128)S(1)} %get-tuple-element.359), channel_id=1, source_target_pairs={{0,1},{1,2},{2,3},{3,4},{4,5},{5,6},{6,7},{7,8},{8,9},{9,10},{10,1... | collective-permute-start | bytes 442376 | tf_op jit(solution)/shard_map/ppermute | solution.py:29
  436.3 3.5 collective-permute-start.11
  438.2 4.1 copy-start.15
  438.2 4.1 copy-start.19
  438.2 4.1 copy-start.21
  438.2 4.1 copy-start.22
  438.2 4.1 copy-start.25
  442.2 1.6 copy-start.17
  570.5 43.2 %copy-start.24 = (f32[144,144]{0,1:T(8,128)S(1)}, f32[144,144]{0,1:T(8,128)}, u32[]{:S(2)}) copy-start(f32[144,144]{0,1:T(8,128)} %get-tuple-element.356) | copy-start | bytes 248836
Sparse Core Ops, SparseCore 0:
  194.2 91.5 all-reduce.10
  445.5 93.7 all-reduce.12
where the time goes:
time: 634 us; the launch traced here: 624 us
  waiting for transfers between devices  193 us (30%)
  blocking collectives  122 us (19%)
  other arithmetic  114 us (18%)
  matrix products  96 us (15%)
  local copies, waits for them, and re-layouts  52.9 us (8%)
  starting transfers between devices  24.7 us (4%)
  between operations  16.8 us (3%)
    psum x2, waiting for transfers between devices, body(): lax.psum((inner(basis, stiff_basis), inner(basis, mass_basis)), 'sub')  186 us
    psum x1, blocking collectives, body(): lax.psum((inner(modes_start, stiff_start), inner(modes_start, mass_start)...  63.9 us
    psum x1, blocking collectives, body(): rayleigh = symmetric(lax.psum(inner(current, stiff_cur), 'sub'))  58.5 us
    another operation x18, other arithmetic, lower_solve(): lax.linalg.triangular_solve(factor, rhs, left_side=True, lower=True, tran...  49.6 us
    another operation x10, other arithmetic, small_step(): factor = jnp.linalg.cholesky(stiff_scaled)  33.8 us
    dot_general x6, matrix products, one_block(): jnp.einsum('ije,rje->rie', stiff_here, picked, precision=highest)  24.3 us
    dot_general x6, matrix products, one_block(): mass_part = jnp.einsum('ije,rje->rie', mass_here, picked, precision=highest)  24.3 us
    another operation x12, other arithmetic, small_step(): small_factor = jnp.linalg.cholesky(normal_gram)  20.2 us
  transfers between devices with their start and end apart: 14, of which 7 were waited for; matrix products, arithmetic and copies ran while one was open for 2% of the time, Pallas kernels for 0%

commit v1 on v0

--- a/solution.py
+++ b/solution.py
@@ -126,7 +126,7 @@
     carried = rayleigh
     for sweep in range(ITERS):
         if sweep > 0:
-            rayleigh = symmetric(lax.psum(inner(current, stiff_cur), "sub"))
+            rayleigh = symmetric(jnp.sum(lax.all_gather(inner(current, stiff_cur), "sub"), axis=0))
         residual = stiff_cur - combine(rayleigh, mass_cur)
         stiff_res, mass_res = apply_pair(residual, stiffness, mass, connect)
         if sweep == 0:

time: 634 us -> 600 us (0.946)
  blocking collectives: 122 us -> 84.4 us
    psum x1 -> x0, blocking collectives: 58.5 us -> none  [body(): rayleigh = symmetric(lax.psum(inner(current, stiff_cur), 'sub'))]
    all_gather x0 -> x1, blocking collectives: none -> 20.5 us  [body(): lax.all_gather(inner(current, stiff_cur), 'sub')]
where the time goes in v1:
time: 600 us; the launch traced here: 590 us
  waiting for transfers between devices  193 us (32%)
  other arithmetic  114 us (19%)
  matrix products  96 us (16%)
  blocking collectives  84.4 us (14%)
  local copies, waits for them, and re-layouts  52.9 us (9%)
  starting transfers between devices  27.9 us (5%)
  between operations  16.8 us (3%)
    psum x2, waiting for transfers between devices, body(): lax.psum((inner(basis, stiff_basis), inner(basis, mass_basis)), 'sub')  186 us
    psum x1, blocking collectives, body(): lax.psum((inner(modes_start, stiff_start), inner(modes_start, mass_start)...  63.9 us
    another operation x18, other arithmetic, lower_solve(): lax.linalg.triangular_solve(factor, rhs, left_side=True, lower=True, tran...  49.6 us
    another operation x10, other arithmetic, small_step(): factor = jnp.linalg.cholesky(stiff_scaled)  33.8 us
    dot_general x6, matrix products, one_block(): jnp.einsum('ije,rje->rie', stiff_here, picked, precision=highest)  24.3 us
    dot_general x6, matrix products, one_block(): mass_part = jnp.einsum('ije,rje->rie', mass_here, picked, precision=highest)  24.2 us
    all_gather x1, blocking collectives, body(): lax.all_gather(inner(current, stiff_cur), 'sub')  20.5 us
    another operation x12, other arithmetic, small_step(): small_factor = jnp.linalg.cholesky(normal_gram)  20.2 us
  transfers between devices with their start and end apart: 14, of which 7 were waited for; matrix products, arithmetic and copies ran while one was open for 2% of the time, Pallas kernels for 0%

profile of v1, /device:TPU:0, one launch (start us, length us, event | category | flops | bytes accessed | tf_op | source)
XLA Modules:
  0.0 589.7 jit_solution(11412868253818242789)
XLA Ops:
  8.3 2.4 collective-permute-start
  12.2 3.1 copy.66
  15.2 2.2 copy.67
  19.5 33.1 %while.45 = (s32[]{:T(128)}, f32[2,48,6,384]{3,1,2,0:T(8,128)}, s32[2]{0:T(128)S(1)}, f32[48,6,384]{2,0,1:T(8,128)}, s32[2,4,128]{2,1,0:T(4,128)S(1)}, /*index=5...) while((s32[]{:T(128)}, f32[2,48,6,384]{3,1,2,0:T(8,128)}, ...), condition=%wide.region_1.2_spmd.clone, body=%wide.region_0.1_spmd.clone.sunk | while | flops 1444594176 | bytes 14656723 | solution.py:97
  20.7 1.5 fusion.318
  22.8 4.0 fusion.320
  28.2 4.0 fusion.319
  33.3 2.7 fusion.321
  37.3 1.5 fusion.318
  39.3 4.0 fusion.320
  44.8 4.0 fusion.319
  49.9 2.7 fusion.321
  53.9 5.2 collective-permute-start.2
  61.3 2.7 collective-permute-done.3
  64.1 2.3 scatter-add.21
  67.2 63.9 %all-reduce.6 = (f32[48,48]{1,0:T(8,128)S(1)}, f32[48,48]{0,1:T(8,128)S(1)}) all-reduce(f32[48,48]{1,0:T(8,128)S(1)} %convolution_bitcast_fusion.9, f32[48,48]{0,1:T(8,128)S(1)} %convolution_bitcast_fusion.8), channel_id=1, replica_groups=mesh['groups'=2,'sub'=16] {'sub'}, use_global_device_ids=true, to_apply=%region_2.3 | all-reduce | flops 4608 | bytes 36864 | tf_op jit(solution)/shard_map/psum | solution.py:112
  131.3 4.4 cholesky.251
  137.0 3.7 custom-call.37
  145.3 1.9 collective-permute-done.5
  148.5 31.3 %while.46 = (s32[]{:T(128)}, f32[2,48,6,384]{3,1,2,0:T(8,128)}, s32[2]{0:T(128)S(1)}, f32[48,6,384]{2,0,1:T(8,128)S(1)}, s32[2,4,128]{2,1,0:T(4,128)S(1)}, /*ind...) while((s32[]{:T(128)}, f32[2,48,6,384]{3,1,2,0:T(8,128)}, ...), condition=%wide.region_7.9_spmd.clone, body=%wide.region_6.8_spmd.clone.sunk | while | flops 1444594176 | bytes 18195724 | solution.py:97
  151.0 4.0 fusion.332
  156.4 4.0 fusion.331
  161.5 2.7 fusion.333
  166.6 4.0 fusion.332
  172.0 4.0 fusion.331
  177.2 2.7 fusion.333
  181.1 2.9 collective-permute-start.6
  185.6 1.5 collective-permute-start.7
  189.3 2.3 scatter-add.25
  194.2 91.6 %all-reduce.11.cloned.1.call-done = (f32[96,96]{0,1:T(8,128)}, f32[96,96]{0,1:T(8,128)}) async-done(((f32[96,96]{0,1:T(8,128)}, f32[96,96]{0,1:T(8,128)}), (f32[96,96]{0,1:T(8,128)}, f32[96,96]{0,1:T(8,128)})) %all-reduce.11.cloned.1.call-update) | async-done | bytes 73744 | tf_op jit(solution)/shard_map/psum | solution.py:140
  285.8 2.2 gather_fusion
  289.3 8.8 %cholesky.95 = f32[96,96]{1,0:T(8,128)S(1)} custom-call(f32[96,96]{1,0:T(8,128)S(1)} %broadcast_multiply_fusion.1), custom_call_target="Cholesky" | custom-call | tf_op jit(solution)/shard_map/jit(cholesky)/cholesky | solution.py:55
  299.4 7.4 %custom-call.55 = f32[1,96,96]{1,2,0:T(8,128)S(1)} custom-call(f32[1,96,96]{2,1,0:T(8,128)S(1)} %fusion.104), custom_call_target="InvertDiagBlocksLowerTriangular" | custom-call | tf_op jit(solution)/shard_map/triangular_solve/custom-call.7 | solution.py:45
  308.1 4.4 cholesky.262
  313.8 3.7 custom-call.53
  319.0 4.4 cholesky.273
  324.7 3.7 custom-call.56
  331.5 20.5 %all-gather = f32[768,48]{1,0:T(8,128)S(1)} all-gather(f32[48,48]{1,0:T(8,128)S(1)} %convolution_bitcast_fusion.7), channel_id=2, replica_groups=mesh['groups'=2,'sub'=16] {'sub'}, dimensions={0}, use_global_device_ids=true | all-gather | bytes 156672 | tf_op jit(solution)/shard_map/all_gather | solution.py:129
  352.7 2.3 collective-permute-start.8
  355.0 1.5 collective-permute-start.9
  360.2 33.2 %while.47 = (s32[]{:T(128)}, f32[2,48,6,384]{3,1,2,0:T(8,128)}, s32[2]{0:T(128)S(1)}, f32[48,6,384]{2,0,1:T(8,128)}, s32[2,4,128]{2,1,0:T(4,128)S(1)}, /*index=5...) while((s32[]{:T(128)}, f32[2,48,6,384]{3,1,2,0:T(8,128)}, ...), condition=%wide.region_14.19_spmd.clone, body=%wide.region_13.18_spmd.clone.sunk | while | flops 1444594176 | bytes 14656723 | solution.py:97
  361.5 1.5 fusion.342
  363.5 4.0 fusion.344
  369.0 4.0 fusion.343
  374.1 2.7 fusion.345
  378.1 1.5 fusion.342
  380.2 4.0 fusion.344
  385.6 4.0 fusion.343
  390.8 2.7 fusion.345
  394.7 5.1 collective-permute-start.10
  401.5 1.7 collective-permute-start.11
  405.1 2.3 scatter-add.29
  407.5 1.5 convolution_bitcast_fusion.3
  409.0 1.5 convolution_bitcast_fusion.4
  410.6 94.1 %all-reduce.13.cloned.1.call-done = (f32[144,144]{0,1:T(8,128)}, f32[144,144]{0,1:T(8,128)}) async-done(((f32[144,144]{0,1:T(8,128)}, f32[144,144]{0,1:T(8,128)}), (f32[144,144]{0,1:T(8,128)}, f32[144,144]{0,1:T(8,128)})) %all-reduce.13.cloned.1.call-update) | async-done | bytes 165904 | tf_op jit(solution)/shard_map/psum | solution.py:140
  504.7 3.2 gather_fusion.1
  509.8 11.7 %cholesky.155 = f32[128,128]{1,0:T(8,128)S(1)} custom-call(f32[128,128]{1,0:T(8,128)S(1)} %cholesky.304), custom_call_target="Cholesky" | custom-call | tf_op jit(solution)/shard_map/jit(cholesky)/cholesky | solution.py:55
  521.6 9.8 %custom-call.38 = f32[1,128,128]{1,2,0:T(8,128)S(1)} custom-call(f32[1,128,128]{2,1,0:T(8,128)S(1)} %get-tuple-element.375), custom_call_target="InvertDiagBlocksLowerTriangular" | custom-call | tf_op jit(solution)/shard_map/jit(cholesky)/cholesky | solution.py:55
  531.7 1.5 cholesky.175
  535.9 19.8 %custom-call.61 = f32[2,128,128]{1,2,0:T(8,128)S(1)} custom-call(f32[2,128,128]{2,1,0:T(8,128)S(1)} %pad_maximum_fusion.17), custom_call_target="InvertDiagBlocksLowerTriangular" | custom-call | tf_op jit(solution)/shard_map/triangular_solve/custom-call.10 | solution.py:45
  557.6 4.4 cholesky.284
  563.4 3.7 custom-call.59
  569.4 4.4 cholesky.295
  575.2 3.7 custom-call.62
  (280 shorter events, 80.8 us)
Async XLA Ops:
  7.2 278.7 %all-reduce.11.cloned.1.call-start = ((), (), s32[]{:S(2)}) async-start(), calls=%async_computation | async-start | bytes 196608 | tf_op jit(solution)/shard_map/psum | solution.py:140
  8.3 9.2 %collective-permute-start = (f32[48,6,64]{2,0,1:T(8,128)S(1)}, f32[48,6,64]{2,0,1:T(8,128)S(1)}, u32[]{:S(2)}, u32[]{:S(2)}) collective-permute-start(f32[48,6,64]{2,0,1:T(8,128)S(1)} %get-tuple-element.372), channel_id=1, source_target_pairs={{0,1},{1,2},{2,3},{3,4},{4,5},{5,6},{6,7},{7,8},{8,9},{9,10},{10,1... | collective-permute-start | bytes 221192 | tf_op jit(solution)/shard_map/ppermute | solution.py:18
  10.7 4.5 copy-start.23
  10.7 6.7 %collective-permute-start.1 = (f32[48,6,64]{2,0,1:T(8,128)S(1)}, f32[48,6,64]{2,0,1:T(8,128)S(1)}, u32[]{:S(2)}, u32[]{:S(2)}) collective-permute-start(f32[48,6,64]{2,0,1:T(8,128)S(1)} %get-tuple-element.373), channel_id=1, source_target_pairs={{1,0},{2,1},{3,2},{4,3},{5,4},{6,5},{7,6},{8,7},{9,8},{10,9},{11,1... | collective-permute-start | bytes 221192 | tf_op jit(solution)/shard_map/ppermute | solution.py:21
  15.2 2.2 copy-start.8
  17.5 2.0 copy-start.26
  32.3 1.1 copy-start
  48.8 1.1 copy-start
  52.6 6.5 %copy-start.3 = (f32[2,48,6,384]{3,1,2,0:T(8,128)S(1)}, f32[2,48,6,384]{3,1,2,0:T(8,128)}, u32[]{:S(2)}) copy-start(f32[2,48,6,384]{3,1,2,0:T(8,128)} %get-tuple-element.207) | copy-start | bytes 2654212
  53.9 6.7 %collective-permute-start.2 = (f32[2,48,6,64]{3,1,2,0:T(8,128)S(1)}, f32[2,48,6,64]{3,1,2,0:T(8,128)S(1)}, u32[]{:S(2)}, u32[]{:S(2)}) collective-permute-start(f32[2,48,6,64]{3,1,2,0:T(8,128)S(1)} %get-tuple-element.363), channel_id=1, source_target_pairs={{0,1},{1,2},{2,3},{3,4},{4,5},{5,6},{6,7},{7,8},{8,9},{9,10},{10,1... | collective-permute-start | bytes 442376 | tf_op jit(solution)/shard_map/ppermute | solution.py:29
  59.3 4.7 collective-permute-start.3
  141.3 6.2 %copy-start.10 = (f32[48,6,256]{2,0,1:T(8,128)}, f32[48,6,256]{2,0,1:T(8,128)S(1)}, u32[]{:S(2)}) copy-start(f32[48,6,256]{2,0,1:T(8,128)S(1)} %fusion.92) | copy-start | bytes 884740
  141.7 6.8 %copy-start.12 = (f32[48,6,256]{2,0,1:T(8,128)}, f32[48,6,256]{2,0,1:T(8,128)S(1)}, u32[]{:S(2)}) copy-start(f32[48,6,256]{2,0,1:T(8,128)S(1)} %fusion.93) | copy-start | bytes 884740
  142.7 2.6 collective-permute-start.4
  144.0 3.3 collective-permute-start.5
  148.5 2.4 copy-start.6
  160.4 1.1 copy-start.1
  161.1 3.1 copy-start.7
  164.2 2.4 copy-start.6
  176.1 1.1 copy-start.1
  176.8 3.1 copy-start.7
  179.9 5.6 copy-start.4
  181.1 6.0 %collective-permute-start.6 = (f32[2,48,6,64]{3,1,2,0:T(8,128)S(1)}, f32[2,48,6,64]{3,1,2,0:T(8,128)S(1)}, u32[]{:S(2)}, u32[]{:S(2)}) collective-permute-start(f32[2,48,6,64]{3,1,2,0:T(8,128)S(1)} %get-tuple-element.361), channel_id=1, source_target_pairs={{0,1},{1,2},{2,3},{3,4},{4,5},{5,6},{6,7},{7,8},{8,9},{9,10},{10,1... | collective-permute-start | bytes 442376 | tf_op jit(solution)/shard_map/ppermute | solution.py:29
  185.6 3.5 collective-permute-start.7
  187.3 4.3 copy-start.13
  189.3 3.6 copy-start.11
  191.5 138.4 %copy-start.9 = (f32[2,48,6,256]{3,1,2,0:T(8,128)}, f32[2,48,6,256]{3,1,2,0:T(8,128)S(1)}, u32[]{:S(2)}) copy-start(f32[2,48,6,256]{3,1,2,0:T(8,128)S(1)} %scatter-add.25) | copy-start | bytes 1769476
  194.1 310.5 %all-reduce.13.cloned.1.call-start = ((), (), s32[]{:S(2)}) async-start(), calls=%async_computation.1 | async-start | bytes 589824 | tf_op jit(solution)/shard_map/psum | solution.py:140
  329.1 22.9 %copy-start.18 = (f32[48,6,256]{2,0,1:T(8,128)}, f32[48,6,256]{2,0,1:T(8,128)S(1)}, u32[]{:S(2)}) copy-start(f32[48,6,256]{2,0,1:T(8,128)S(1)} %fusion.90) | copy-start | bytes 884740
  329.5 23.0 %copy-start.16 = (f32[48,6,256]{2,0,1:T(8,128)}, f32[48,6,256]{2,0,1:T(8,128)S(1)}, u32[]{:S(2)}) copy-start(f32[48,6,256]{2,0,1:T(8,128)S(1)} %fusion.89) | copy-start | bytes 884740
  330.0 22.7 %copy-start.20 = (f32[48,6,256]{2,0,1:T(8,128)}, f32[48,6,256]{2,0,1:T(8,128)S(1)}, u32[]{:S(2)}) copy-start(f32[48,6,256]{2,0,1:T(8,128)S(1)} %fusion.88) | copy-start | bytes 884740
  352.6 5.7 copy-start.14
  352.7 4.9 collective-permute-start.8
  355.0 3.3 collective-permute-start.9
  373.1 1.1 copy-start.2
  389.7 1.1 copy-start.2
  393.5 7.8 %copy-start.5 = (f32[2,48,6,384]{3,1,2,0:T(8,128)S(1)}, f32[2,48,6,384]{3,1,2,0:T(8,128)}, u32[]{:S(2)}) copy-start(f32[2,48,6,384]{3,1,2,0:T(8,128)} %get-tuple-element.209) | copy-start | bytes 2654212
  394.7 8.5 %collective-permute-start.10 = (f32[2,48,6,64]{3,1,2,0:T(8,128)S(1)}, f32[2,48,6,64]{3,1,2,0:T(8,128)S(1)}, u32[]{:S(2)}, u32[]{:S(2)}) collective-permute-start(f32[2,48,6,64]{3,1,2,0:T(8,128)S(1)} %get-tuple-element.359), channel_id=1, source_target_pairs={{0,1},{1,2},{2,3},{3,4},{4,5},{5,6},{6,7},{7,8},{8,9},{9,10},{10,1... | collective-permute-start | bytes 442376 | tf_op jit(solution)/shard_map/ppermute | solution.py:29
  401.5 3.5 collective-permute-start.11
  403.4 4.1 copy-start.15
  403.4 4.1 copy-start.19
  403.4 4.1 copy-start.21
  403.4 4.1 copy-start.22
  403.4 4.1 copy-start.25
  407.4 1.6 copy-start.17
  535.9 43.2 %copy-start.24 = (f32[144,144]{0,1:T(8,128)S(1)}, f32[144,144]{0,1:T(8,128)}, u32[]{:S(2)}) copy-start(f32[144,144]{0,1:T(8,128)} %get-tuple-element.356) | copy-start | bytes 248836
Sparse Core Ops, SparseCore 0:
  194.2 91.5 all-reduce.10
  410.7 93.9 all-reduce.12
